TPU v7x, 32 devices: a whole 2x2x4 slice. The times are simulated.
32 devices in a mesh: row: 8 (over y, x, core), col: 4 (over z).
Axes of the slice: x: 2, y: 2, z: 4, core: 2. Of those that a mesh axis runs over, the one named last changes fastest.
Arguments:
- tile_values: bfloat16 [8, 4, 64, 128, 128], P('row', 'col'), may hold values from -0.0625 to 0.0625
- tile_row: int32 [8, 4, 64], P('row', 'col'), may hold values from 0 to 3
- tile_col: int32 [8, 4, 64], P('row', 'col'), may hold values from 0 to 3
- tile_count: int32 [8, 4], P('row', 'col'), may hold values from 16 to 64, as said below
- primal_init: float32 [64, 2048], P(None, ('row', 'col')), may hold values from -3 to 3
- dual_init: float32 [64, 4096], P(None, ('row', 'col')), may hold values from -3 to 3
- cost_vector: float32 [2048], P(('row', 'col')), may hold values from -4 to 4
- lower_bound: float32 [2048], P(('row', 'col')), may hold values from -1 to -0.2
- upper_bound: float32 [2048], P(('row', 'col')), may hold values from 0.2 to 1
- bound_kind: int32 [2048], P(('row', 'col')), may hold values from 0 to 2
- row_kind: int32 [4096], P(('row', 'col')), may hold values from 0 to 1
- demand: float32 [64, 4096], P(None, ('row', 'col')), may hold values from -20 to 20
Outputs:
- primal_out: float32 [64, 2048], P(None, ('row', 'col'))
- dual_out: float32 [64, 4096], P(None, ('row', 'col'))
- residual_norm: float32 [3, 64], replicated
Inputs may be any that keep to these rules, and one draw needn't show every extreme that they name: `tile_count`: live tile slots of one device; some device has all 64 slots live.
All inputs are finite; a program needn't handle non-finite values.
Results may differ from a plain program's by a relative error of at most 0.0022.
Values may be sent and summed in bfloat16 or wider, within the bound.
A program may use at most 64 MiB of HBM per device.

v0:
```python
import jax
import jax.numpy as jnp
from jax import lax
from jax.sharding import PartitionSpec as P

ITERS = 3
PRIMAL_STEP = 0.4
DUAL_STEP = 0.4
NORM_EPS = 1e-06


def block_sum(onehot, product):
    return jnp.einsum("tr,sti->sri", onehot, product, precision=lax.Precision.HIGHEST)


def shards(
    tile_values,
    tile_row,
    tile_col,
    tile_count,
    primal_init,
    dual_init,
    cost_vector,
    lower_bound,
    upper_bound,
    bound_kind,
    row_kind,
    demand,
):
    blocks = tile_values[0, 0]
    slot_rows = tile_row[0, 0]
    slot_cols = tile_col[0, 0]
    live_count = tile_count[0, 0]
    slots = blocks.shape[0]
    tile_size = blocks.shape[-1]
    scenarios = primal_init.shape[0]
    row_devices = lax.axis_size("row")
    col_devices = lax.axis_size("col")
    col_blocks = row_devices // 2
    live_mask = jnp.arange(slots, dtype=jnp.int32) < live_count
    row_onehot = (
        (slot_rows[:, None] == jnp.arange(col_devices, dtype=jnp.int32)[None, :])
        & live_mask[:, None]
    ).astype(jnp.float32)
    col_onehot = (
        (slot_cols[:, None] == jnp.arange(col_blocks, dtype=jnp.int32)[None, :])
        & live_mask[:, None]
    ).astype(jnp.float32)
    total_rows = row_devices * col_devices * tile_size
    inequality = (row_kind == 1).astype(jnp.float32)
    primal = primal_init
    dual = dual_init
    partial_norms = []
    for iteration in range(ITERS):
        dual_half = lax.all_gather(dual.astype(jnp.bfloat16), "col", axis=1, tiled=True)
        grouped = dual_half.reshape(scenarios, col_devices, tile_size)
        picked = jnp.take(grouped, slot_rows, axis=1)
        product = jnp.einsum("tij,sti->stj", blocks, picked, preferred_element_type=jnp.float32)
        summed = block_sum(col_onehot, product)
        summed = summed.reshape(scenarios, col_blocks * tile_size)
        transposed = lax.psum_scatter(summed, "row", scatter_dimension=1, tiled=True)
        primal_next = primal - PRIMAL_STEP * (cost_vector[None, :] - transposed)
        primal_next = jnp.where(
            (bound_kind <= 1)[None, :], jnp.maximum(primal_next, lower_bound[None, :]), primal_next
        )
        primal_next = jnp.where(
            (bound_kind == 0)[None, :], jnp.minimum(primal_next, upper_bound[None, :]), primal_next
        )
        extrapolated = (2.0 * primal_next - primal).astype(jnp.bfloat16)
        gathered = lax.all_gather(extrapolated, "row", axis=1, tiled=True)
        apply_grouped = gathered.reshape(scenarios, col_blocks, tile_size)
        apply_picked = jnp.take(apply_grouped, slot_cols, axis=1)
        apply_product = jnp.einsum(
            "tij,stj->sti", blocks, apply_picked, preferred_element_type=jnp.float32
        )
        apply_summed = block_sum(row_onehot, apply_product)
        partial_value = apply_summed.reshape(scenarios, col_devices * tile_size)
        image = lax.psum_scatter(partial_value, "col", scatter_dimension=1, tiled=True)
        gap_rows = demand - image
        dual = dual + DUAL_STEP * gap_rows
        dual = jnp.where(inequality[None, :] > 0.0, jnp.maximum(dual, 0.0), dual)
        primal = primal_next
        squares = jnp.sum(gap_rows * gap_rows, axis=1)
        partial_norms.append(lax.psum(squares, ("row", "col")))
    totals = jnp.stack(partial_norms)
    residual_norm = jnp.sqrt(totals / total_rows + NORM_EPS)
    return (primal, dual, residual_norm)


def solution(mesh):
    return jax.shard_map(
        shards,
        mesh=mesh,
        in_specs=(
            P("row", "col", None, None, None),
            P("row", "col", None),
            P("row", "col", None),
            P("row", "col"),
            P(None, ("row", "col")),
            P(None, ("row", "col")),
            P(("row", "col")),
            P(("row", "col")),
            P(("row", "col")),
            P(("row", "col")),
            P(("row", "col")),
            P(None, ("row", "col")),
        ),
        out_specs=(P(None, ("row", "col")), P(None, ("row", "col")), P()),
        check_vma=False,
    )
```

profile of v0, /device:TPU:10, one launch (start us, length us, event | category | flops | bytes accessed | tf_op | source)
XLA Modules:
  0.0 312.5 jit_solution(8858715847128932885)
XLA Ops:
  10.1 12.3 %all_gather.18 = bf16[64,512]{1,0:T(8,128)(2,1)S(1)} all-gather(bf16[64,128]{1,0:T(8,128)(2,1)S(1)} %convert_element_type.23), channel_id=1, replica_groups=mesh['row'=8,'col'=4] {'col'}, dimensions={1}, use_global_device_ids=true | all-gather | bytes 81920 | tf_op jit(solution)/shard_map/all_gather | solution.py:55
  24.1 2.0 fusion.42
  27.0 33.3 %reduce-scatter.19.cloned.1.call-done = f32[64,64]{1,0:T(8,128)} async-done(((f32[512,64]{1,0:T(8,128)}), f32[64,64]{1,0:T(8,128)}) %reduce-scatter.19.cloned.1.call-update) | async-done | bytes 16400
  61.3 8.3 %all_gather.19 = bf16[64,512]{0,1:T(8,128)(2,1)S(1)} all-gather(bf16[64,64]{0,1:T(8,128)(2,1)S(1)} %copy.29), channel_id=1, replica_groups=mesh['row'=8,'col'=4] {'row'}, dimensions={1}, use_global_device_ids=true | all-gather | bytes 73728 | tf_op jit(solution)/shard_map/all_gather | solution.py:70
  70.5 1.5 fusion.27
  72.1 2.0 fusion.20
  74.8 17.4 %reduce-scatter.13.cloned.1.call-done = f32[64,128]{1,0:T(8,128)} async-done(((f32[64,512]{1,0:T(8,128)}), f32[64,128]{1,0:T(8,128)}) %reduce-scatter.13.cloned.1.call-update) | async-done | bytes 32784 | tf_op jit(solution)/shard_map/reduce_scatter | solution.py:78
  93.0 12.4 %all_gather.20 = bf16[64,512]{1,0:T(8,128)(2,1)S(1)} all-gather(bf16[64,128]{1,0:T(8,128)(2,1)S(1)} %fusion.75), channel_id=1, replica_groups=mesh['row'=8,'col'=4] {'col'}, dimensions={1}, use_global_device_ids=true | all-gather | bytes 81920 | tf_op jit(solution)/shard_map/all_gather | solution.py:55
  106.9 2.0 fusion.45
  108.8 0.8 copy.58
  109.8 34.5 %reduce-scatter.21.cloned.1.call-done = f32[64,64]{1,0:T(8,128)} async-done(((f32[512,64]{1,0:T(8,128)}), f32[64,64]{1,0:T(8,128)}) %reduce-scatter.21.cloned.1.call-update) | async-done | bytes 16400
  145.2 8.5 %all_gather.21 = bf16[64,512]{0,1:T(8,128)(2,1)S(1)} all-gather(bf16[64,64]{0,1:T(8,128)(2,1)S(1)} %copy.35), channel_id=1, replica_groups=mesh['row'=8,'col'=4] {'row'}, dimensions={1}, use_global_device_ids=true | all-gather | bytes 73728 | tf_op jit(solution)/shard_map/all_gather | solution.py:70
  154.5 1.5 fusion.33
  156.1 2.0 fusion.16
  158.8 17.4 %reduce-scatter.15.cloned.1.call-done = f32[64,128]{1,0:T(8,128)} async-done(((f32[64,512]{1,0:T(8,128)}), f32[64,128]{1,0:T(8,128)}) %reduce-scatter.15.cloned.1.call-update) | async-done | bytes 32784 | tf_op jit(solution)/shard_map/reduce_scatter | solution.py:78
  177.0 12.4 %all_gather.22 = bf16[64,512]{1,0:T(8,128)(2,1)S(1)} all-gather(bf16[64,128]{1,0:T(8,128)(2,1)S(1)} %fusion.95), channel_id=1, replica_groups=mesh['row'=8,'col'=4] {'col'}, dimensions={1}, use_global_device_ids=true | all-gather | bytes 81920 | tf_op jit(solution)/shard_map/all_gather | solution.py:55
  190.9 2.0 fusion.48
  193.8 34.5 %reduce-scatter.23.cloned.1.call-done = f32[64,64]{1,0:T(8,128)} async-done(((f32[512,64]{1,0:T(8,128)}), f32[64,64]{1,0:T(8,128)}) %reduce-scatter.23.cloned.1.call-update) | async-done | bytes 16400
  229.8 8.3 %all_gather.23 = bf16[64,512]{0,1:T(8,128)(2,1)S(1)} all-gather(bf16[64,64]{0,1:T(8,128)(2,1)S(1)} %copy.41), channel_id=1, replica_groups=mesh['row'=8,'col'=4] {'row'}, dimensions={1}, use_global_device_ids=true | all-gather | bytes 73728 | tf_op jit(solution)/shard_map/all_gather | solution.py:70
  239.0 1.5 fusion.39
  240.5 2.0 fusion.12
  243.1 17.5 %reduce-scatter.17.cloned.1.call-done = f32[64,128]{1,0:T(8,128)} async-done(((f32[64,512]{1,0:T(8,128)}), f32[64,128]{1,0:T(8,128)}) %reduce-scatter.17.cloned.1.call-update) | async-done | bytes 32784 | tf_op jit(solution)/shard_map/reduce_scatter | solution.py:78
  260.6 1.5 multiply_reduce_fusion.2
  262.1 42.9 %all-reduce = (f32[1,64]{1,0:T(1,128)S(1)}, f32[1,64]{1,0:T(1,128)S(1)}, f32[1,64]{1,0:T(1,128)S(1)}) all-reduce(f32[1,64]{1,0:T(1,128)S(1)} %bitcast.152, f32[1,64]{1,0:T(1,128)S(1)} %bitcast.151, f32[1,64]{1,0:T(1,128)S(1)} %bitcast.150), channel_id=1, replica_groups=mesh['row'=8,'col'=4] {'row','col'}, use_global_device_ids=true, to_apply=%region_11.13 | all-reduce | flops 192 | bytes 1536 | tf_op jit(solution)/shard_map/psum | solution.py:84
  (80 shorter events, 19.0 us)
Async XLA Ops:
  7.2 16.1 %copy-start = (bf16[1,1,64,128,128]{4,3,2,1,0:T(8,128)(2,1)S(1)}, bf16[1,1,64,128,128]{4,3,2,1,0:T(8,128)(2,1)}, u32[]{:S(2)}) copy-start(bf16[1,1,64,128,128]{4,3,2,1,0:T(8,128)(2,1)} %param.14) | copy-start | bytes 6291460
  7.2 53.1 %reduce-scatter.19.cloned.1.call-start = ((), (), s32[]{:S(2)}) async-start(), calls=%async_computation.9 | async-start | bytes 294912
  23.3 0.8 copy-start.9
  24.0 3.0 copy-start.11
  24.0 37.2 %copy-start.4 = (f32[64,64]{1,0:T(8,128)S(1)}, f32[64,64]{1,0:T(8,128)}, u32[]{:S(2)}) copy-start(f32[64,64]{1,0:T(8,128)} %param.18) | copy-start | bytes 49156
  24.0 37.1 %copy-start.6 = (f32[64]{0:T(128)S(1)}, f32[64]{0:T(128)}, u32[]{:S(2)}) copy-start(f32[64]{0:T(128)} %param.22) | copy-start | bytes 772
  24.0 37.1 %copy-start.7 = (f32[64]{0:T(128)S(1)}, f32[64]{0:T(128)}, u32[]{:S(2)}) copy-start(f32[64]{0:T(128)} %param.21) | copy-start | bytes 772
  24.0 37.1 %copy-start.8 = (f32[64]{0:T(128)S(1)}, f32[64]{0:T(128)}, u32[]{:S(2)}) copy-start(f32[64]{0:T(128)} %param.20) | copy-start | bytes 772
  26.9 65.3 %reduce-scatter.13.cloned.1.call-start = ((), (), s32[]{:S(2)}) async-start(), calls=%async_computation.6 | async-start | bytes 163840 | tf_op jit(solution)/shard_map/reduce_scatter | solution.py:78
  70.5 1.6 copy-start.10
  72.0 2.7 copy-start.12
  72.0 20.1 %copy-start.1 = (f32[64,128]{1,0:T(8,128)S(1)}, f32[64,128]{1,0:T(8,128)}, u32[]{:S(2)}) copy-start(f32[64,128]{1,0:T(8,128)} %param.19) | copy-start | bytes 98308
  72.1 20.1 %copy-start.2 = (f32[64,128]{1,0:T(8,128)S(1)}, f32[64,128]{1,0:T(8,128)}, u32[]{:S(2)}) copy-start(f32[64,128]{1,0:T(8,128)} %param.25) | copy-start | bytes 98308
  74.7 69.5 %reduce-scatter.21.cloned.1.call-start = ((), (), s32[]{:S(2)}) async-start(), calls=%async_computation.10 | async-start | bytes 294912
  109.7 66.5 %reduce-scatter.15.cloned.1.call-start = ((), (), s32[]{:S(2)}) async-start(), calls=%async_computation.7 | async-start | bytes 163840 | tf_op jit(solution)/shard_map/reduce_scatter | solution.py:78
  156.1 20.1 %copy-start.3 = (f32[64,128]{1,0:T(8,128)S(1)}, f32[64,128]{1,0:T(8,128)}, u32[]{:S(2)}) copy-start(f32[64,128]{1,0:T(8,128)} %reduce-scatter.13.cloned.1.call-done) | copy-start | bytes 98308
  158.7 69.5 %reduce-scatter.23.cloned.1.call-start = ((), (), s32[]{:S(2)}) async-start(), calls=%async_computation.11 | async-start | bytes 294912
  193.7 66.9 %reduce-scatter.17.cloned.1.call-start = ((), (), s32[]{:S(2)}) async-start(), calls=%async_computation.8 | async-start | bytes 163840 | tf_op jit(solution)/shard_map/reduce_scatter | solution.py:78
  240.5 20.1 %copy-start.5 = (f32[64,128]{1,0:T(8,128)S(1)}, f32[64,128]{1,0:T(8,128)}, u32[]{:S(2)}) copy-start(f32[64,128]{1,0:T(8,128)} %reduce-scatter.15.cloned.1.call-done) | copy-start | bytes 98308
Sparse Core Ops, SparseCore 0:
  27.0 33.2 reduce-scatter.18
  74.8 17.2 reduce-scatter.12
  109.8 34.3 reduce-scatter.20
  158.9 17.2 reduce-scatter.14
  193.8 34.3 reduce-scatter.22
  243.3 17.2 reduce-scatter.16
where the time goes:
time: 313 us
  waiting for transfers between devices  155 us (50%)
  blocking collectives  105 us (34%)
  matrix products  18.5 us (6%)
  between operations  15.1 us (5%)
  local copies, waits for them, and re-layouts  12.2 us (4%)
  other arithmetic  6.66 us (2%)
    unnamed x9, waiting for transfers between devices  102 us
    reduce_scatter x3, waiting for transfers between devices, shards(): lax.psum_scatter(partial_value, 'col', scatter_dimension=1, tiled=True)  52.2 us
    psum x1, blocking collectives, shards(): partial_norms.append(lax.psum(squares, ('row', 'col')))  42.9 us
    all_gather x3, blocking collectives, shards(): lax.all_gather(dual.astype(jnp.bfloat16), 'col', axis=1, tiled=True)  37.2 us
    all_gather x3, blocking collectives, shards(): gathered = lax.all_gather(extrapolated, 'row', axis=1, tiled=True)  25.1 us
    dot_general x6, matrix products, block_sum(): jnp.einsum('tr,sti->sri', onehot, product, precision=lax.Precision.HIGHEST)  11.8 us
    unnamed x35, local copies, waits for them, and re-layouts  7.05 us
  transfers between devices with their start and end apart: 6, of which 6 were waited for; matrix products, arithmetic and copies ran while one was open for 0% of the time, Pallas kernels for 0%

commit v1 on v0

--- a/solution.py
+++ b/solution.py
@@ -81,7 +81,7 @@
         dual = jnp.where(inequality[None, :] > 0.0, jnp.maximum(dual, 0.0), dual)
         primal = primal_next
         squares = jnp.sum(gap_rows * gap_rows, axis=1)
-        partial_norms.append(lax.psum(squares, ("row", "col")))
+        partial_norms.append(jnp.sum(lax.all_gather(squares, ("row", "col")), axis=0))
     totals = jnp.stack(partial_norms)
     residual_norm = jnp.sqrt(totals / total_rows + NORM_EPS)
     return (primal, dual, residual_norm)

time: 313 us -> 314 us (level)
    psum x1 -> x0, blocking collectives: 42.9 us -> none  [shards(): partial_norms.append(lax.psum(squares, ('row', 'col')))]
    unnamed x0 -> x1, blocking collectives: none -> 42.9 us
    unnamed x35 -> x41, local copies, waits for them, and re-layouts: 7.05 us -> 7.81 us
where the time goes in v1:
time: 314 us
  waiting for transfers between devices  155 us (49%)
  blocking collectives  105 us (33%)
  matrix products  18.6 us (6%)
  between operations  15.1 us (5%)
  local copies, waits for them, and re-layouts  13.1 us (4%)
  other arithmetic  6.74 us (2%)
    unnamed x9, waiting for transfers between devices  102 us
    reduce_scatter x3, waiting for transfers between devices, shards(): lax.psum_scatter(partial_value, 'col', scatter_dimension=1, tiled=True)  52.2 us
    unnamed x1, blocking collectives  42.9 us
    all_gather x3, blocking collectives, shards(): lax.all_gather(dual.astype(jnp.bfloat16), 'col', axis=1, tiled=True)  37.2 us
    all_gather x3, blocking collectives, shards(): gathered = lax.all_gather(extrapolated, 'row', axis=1, tiled=True)  25.1 us
    dot_general x6, matrix products, block_sum(): jnp.einsum('tr,sti->sri', onehot, product, precision=lax.Precision.HIGHEST)  11.8 us
    unnamed x41, local copies, waits for them, and re-layouts  7.81 us
  transfers between devices with their start and end apart: 6, of which 6 were waited for; matrix products, arithmetic and copies ran while one was open for 0% of the time, Pallas kernels for 0%

profile of v1, /device:TPU:10, one launch (start us, length us, event | category | flops | bytes accessed | tf_op | source)
XLA Modules:
  0.0 313.6 jit_solution(4479882083796330905)
XLA Ops:
  10.1 12.3 %all_gather.36 = bf16[64,512]{1,0:T(8,128)(2,1)S(1)} all-gather(bf16[64,128]{1,0:T(8,128)(2,1)S(1)} %convert_element_type.23), channel_id=1, replica_groups=mesh['row'=8,'col'=4] {'col'}, dimensions={1}, use_global_device_ids=true | all-gather | bytes 81920 | tf_op jit(solution)/shard_map/all_gather | solution.py:55
  24.1 2.0 fusion.42
  27.0 33.3 %reduce-scatter.19.cloned.1.call-done = f32[64,64]{1,0:T(8,128)} async-done(((f32[512,64]{1,0:T(8,128)}), f32[64,64]{1,0:T(8,128)}) %reduce-scatter.19.cloned.1.call-update) | async-done | bytes 16400
  61.3 8.3 %all_gather.37 = bf16[64,512]{0,1:T(8,128)(2,1)S(1)} all-gather(bf16[64,64]{0,1:T(8,128)(2,1)S(1)} %copy.47), channel_id=1, replica_groups=mesh['row'=8,'col'=4] {'row'}, dimensions={1}, use_global_device_ids=true | all-gather | bytes 73728 | tf_op jit(solution)/shard_map/all_gather | solution.py:70
  70.5 1.5 fusion.27
  72.1 2.0 fusion.20
  74.8 17.4 %reduce-scatter.13.cloned.1.call-done = f32[64,128]{1,0:T(8,128)} async-done(((f32[64,512]{1,0:T(8,128)}), f32[64,128]{1,0:T(8,128)}) %reduce-scatter.13.cloned.1.call-update) | async-done | bytes 32784 | tf_op jit(solution)/shard_map/reduce_scatter | solution.py:78
  92.9 12.4 %all_gather.38 = bf16[64,512]{1,0:T(8,128)(2,1)S(1)} all-gather(bf16[64,128]{1,0:T(8,128)(2,1)S(1)} %fusion.75), channel_id=1, replica_groups=mesh['row'=8,'col'=4] {'col'}, dimensions={1}, use_global_device_ids=true | all-gather | bytes 81920 | tf_op jit(solution)/shard_map/all_gather | solution.py:55
  106.9 2.0 fusion.45
  108.8 0.8 copy.76
  109.7 34.5 %reduce-scatter.21.cloned.1.call-done = f32[64,64]{1,0:T(8,128)} async-done(((f32[512,64]{1,0:T(8,128)}), f32[64,64]{1,0:T(8,128)}) %reduce-scatter.21.cloned.1.call-update) | async-done | bytes 16400
  145.2 8.5 %all_gather.39 = bf16[64,512]{0,1:T(8,128)(2,1)S(1)} all-gather(bf16[64,64]{0,1:T(8,128)(2,1)S(1)} %copy.53), channel_id=1, replica_groups=mesh['row'=8,'col'=4] {'row'}, dimensions={1}, use_global_device_ids=true | all-gather | bytes 73728 | tf_op jit(solution)/shard_map/all_gather | solution.py:70
  154.5 1.5 fusion.33
  156.1 2.0 fusion.16
  158.8 17.4 %reduce-scatter.15.cloned.1.call-done = f32[64,128]{1,0:T(8,128)} async-done(((f32[64,512]{1,0:T(8,128)}), f32[64,128]{1,0:T(8,128)}) %reduce-scatter.15.cloned.1.call-update) | async-done | bytes 32784 | tf_op jit(solution)/shard_map/reduce_scatter | solution.py:78
  176.9 12.4 %all_gather.40 = bf16[64,512]{1,0:T(8,128)(2,1)S(1)} all-gather(bf16[64,128]{1,0:T(8,128)(2,1)S(1)} %fusion.95), channel_id=1, replica_groups=mesh['row'=8,'col'=4] {'col'}, dimensions={1}, use_global_device_ids=true | all-gather | bytes 81920 | tf_op jit(solution)/shard_map/all_gather | solution.py:55
  190.9 2.0 fusion.48
  193.7 34.6 %reduce-scatter.23.cloned.1.call-done = f32[64,64]{1,0:T(8,128)} async-done(((f32[512,64]{1,0:T(8,128)}), f32[64,64]{1,0:T(8,128)}) %reduce-scatter.23.cloned.1.call-update) | async-done | bytes 16400
  229.9 8.3 %all_gather.41 = bf16[64,512]{0,1:T(8,128)(2,1)S(1)} all-gather(bf16[64,64]{0,1:T(8,128)(2,1)S(1)} %copy.59), channel_id=1, replica_groups=mesh['row'=8,'col'=4] {'row'}, dimensions={1}, use_global_device_ids=true | all-gather | bytes 73728 | tf_op jit(solution)/shard_map/all_gather | solution.py:70
  239.0 1.5 fusion.39
  240.6 2.0 fusion.12
  243.2 17.4 %reduce-scatter.17.cloned.1.call-done = f32[64,128]{1,0:T(8,128)} async-done(((f32[64,512]{1,0:T(8,128)}), f32[64,128]{1,0:T(8,128)}) %reduce-scatter.17.cloned.1.call-update) | async-done | bytes 32784 | tf_op jit(solution)/shard_map/reduce_scatter | solution.py:78
  260.7 1.5 multiply_reduce_fusion.2
  263.0 42.9 %all-reduce.3 = (f32[2048]{0:T(1024)S(1)}, f32[2048]{0:T(1024)S(1)}, f32[2048]{0:T(1024)S(1)}) all-reduce(f32[2048]{0:T(1024)S(1)} %dynamic-update-slice.2, f32[2048]{0:T(1024)S(1)} %dynamic-update-slice.1, f32[2048]{0:T(1024)S(1)} %dynamic-update-slice), channel_id=4, replica_groups=mesh['row'=8,'col'=4] {'row','col'}, use_global_device_ids=true, to_apply=%add.2 | all-reduce | flops 6144 | bytes 49152
  (92 shorter events, 20.0 us)
Async XLA Ops:
  7.2 16.1 %copy-start = (bf16[1,1,64,128,128]{4,3,2,1,0:T(8,128)(2,1)S(1)}, bf16[1,1,64,128,128]{4,3,2,1,0:T(8,128)(2,1)}, u32[]{:S(2)}) copy-start(bf16[1,1,64,128,128]{4,3,2,1,0:T(8,128)(2,1)} %param.14) | copy-start | bytes 6291460
  7.2 53.1 %reduce-scatter.19.cloned.1.call-start = ((), (), s32[]{:S(2)}) async-start(), calls=%async_computation.9 | async-start | bytes 294912
  23.3 0.8 copy-start.9
  24.0 3.0 copy-start.11
  24.0 37.1 %copy-start.4 = (f32[64,64]{1,0:T(8,128)S(1)}, f32[64,64]{1,0:T(8,128)}, u32[]{:S(2)}) copy-start(f32[64,64]{1,0:T(8,128)} %param.18) | copy-start | bytes 49156
  24.0 37.1 %copy-start.6 = (f32[64]{0:T(128)S(1)}, f32[64]{0:T(128)}, u32[]{:S(2)}) copy-start(f32[64]{0:T(128)} %param.22) | copy-start | bytes 772
  24.0 37.1 %copy-start.7 = (f32[64]{0:T(128)S(1)}, f32[64]{0:T(128)}, u32[]{:S(2)}) copy-start(f32[64]{0:T(128)} %param.21) | copy-start | bytes 772
  24.0 37.1 %copy-start.8 = (f32[64]{0:T(128)S(1)}, f32[64]{0:T(128)}, u32[]{:S(2)}) copy-start(f32[64]{0:T(128)} %param.20) | copy-start | bytes 772
  26.9 65.3 %reduce-scatter.13.cloned.1.call-start = ((), (), s32[]{:S(2)}) async-start(), calls=%async_computation.6 | async-start | bytes 163840 | tf_op jit(solution)/shard_map/reduce_scatter | solution.py:78
  70.5 1.6 copy-start.10
  72.0 2.7 copy-start.12
  72.0 20.1 %copy-start.1 = (f32[64,128]{1,0:T(8,128)S(1)}, f32[64,128]{1,0:T(8,128)}, u32[]{:S(2)}) copy-start(f32[64,128]{1,0:T(8,128)} %param.19) | copy-start | bytes 98308
  72.1 20.1 %copy-start.2 = (f32[64,128]{1,0:T(8,128)S(1)}, f32[64,128]{1,0:T(8,128)}, u32[]{:S(2)}) copy-start(f32[64,128]{1,0:T(8,128)} %param.25) | copy-start | bytes 98308
  74.7 69.5 %reduce-scatter.21.cloned.1.call-start = ((), (), s32[]{:S(2)}) async-start(), calls=%async_computation.10 | async-start | bytes 294912
  109.7 66.5 %reduce-scatter.15.cloned.1.call-start = ((), (), s32[]{:S(2)}) async-start(), calls=%async_computation.7 | async-start | bytes 163840 | tf_op jit(solution)/shard_map/reduce_scatter | solution.py:78
  156.1 20.1 %copy-start.3 = (f32[64,128]{1,0:T(8,128)S(1)}, f32[64,128]{1,0:T(8,128)}, u32[]{:S(2)}) copy-start(f32[64,128]{1,0:T(8,128)} %reduce-scatter.13.cloned.1.call-done) | copy-start | bytes 98308
  158.7 69.6 %reduce-scatter.23.cloned.1.call-start = ((), (), s32[]{:S(2)}) async-start(), calls=%async_computation.11 | async-start | bytes 294912
  193.7 67.0 %reduce-scatter.17.cloned.1.call-start = ((), (), s32[]{:S(2)}) async-start(), calls=%async_computation.8 | async-start | bytes 163840 | tf_op jit(solution)/shard_map/reduce_scatter | solution.py:78
  240.6 20.1 %copy-start.5 = (f32[64,128]{1,0:T(8,128)S(1)}, f32[64,128]{1,0:T(8,128)}, u32[]{:S(2)}) copy-start(f32[64,128]{1,0:T(8,128)} %reduce-scatter.15.cloned.1.call-done) | copy-start | bytes 98308
Sparse Core Ops, SparseCore 0:
  27.0 33.2 reduce-scatter.18
  74.8 17.2 reduce-scatter.12
  109.8 34.3 reduce-scatter.20
  158.8 17.2 reduce-scatter.14
  193.8 34.4 reduce-scatter.22
  243.3 17.2 reduce-scatter.16
